TPU v7x, 256 devices: a whole 4x4x8 slice. The times are simulated.
256 devices in a mesh: tm: 256 (over y, z, x, core).
Axes of the slice: x: 4, y: 4, z: 8, core: 2. Of those that a mesh axis runs over, the one named last changes fastest.
Arguments:
- step_ops: float32 [512, 256, 256], P('tm')
- sources: float32 [512, 256], P('tm'), may hold values from -0.3 to 0.3
- terminal: float32 [256], replicated, may hold values from -6 to 6
- inertia_jac: float32 [512, 64], P('tm')
- gen_bus: int32 [64], replicated, may hold values from 0 to 255, as said below
Outputs:
- adjoint_states: float32 [512, 256], P('tm')
- sensitivity: float32 [64], replicated
Inputs may be any that keep to these rules, and one draw needn't show every extreme that they name: `gen_bus`: the 64 entries are distinct state indices.
All inputs are finite; a program needn't handle non-finite values.
Results may differ from a plain program's by a relative error of at most 0.0003.
Values sent between devices are 32-bit elements; how exact they have to be, the bound alone decides.
No kernel may reach another device: no remote copies, remote signals or barrier semaphores. Data moves between devices by JAX's collectives and lax.ppermute only.
A program may use at most 256 MiB of HBM per device.

v0:
```python
import jax
import jax.numpy as jnp
from jax import lax
from jax.sharding import PartitionSpec as P


def prefix_2(value, axis, join, neutral):
    count, mine = (lax.axis_size(axis), lax.axis_index(axis))
    pieces = jax.tree.map(lambda part: lax.all_gather(part, axis), value)
    pieces = jax.tree.map(lambda part: part[::-1], pieces)
    mine = count - 1 - mine
    running = jax.tree.map(
        lambda part, zero: jnp.full_like(part, 0) + jnp.asarray(zero, part.dtype), value, neutral
    )

    def turn(position, running):
        longer = join(running, jax.tree.map(lambda part: part[position], pieces))
        return jax.tree.map(lambda new, old: jnp.where(position < mine, new, old), longer, running)

    return lax.fori_loop(0, count - 1, turn, running)


def matmul(left, right):
    return jnp.dot(left, right, precision=lax.Precision.HIGHEST, preferred_element_type=jnp.float32)


def combine(earlier, later):
    return (matmul(later[0], earlier[0]), matmul(later[0], earlier[1]) + later[1])


def on_device(step_ops, sources, terminal, inertia_jac, gen_bus):
    steps_here = step_ops.shape[0]
    width = step_ops.shape[1]
    block_map = step_ops[steps_here - 1]
    block_vec = sources[steps_here - 1]
    time_increment = 0
    block_map = matmul(step_ops[time_increment], block_map)
    block_vec = matmul(step_ops[time_increment], block_vec) + sources[time_increment]
    identity = (jnp.eye(width, dtype=jnp.float32), jnp.zeros((width,), jnp.float32))
    prefix = prefix_2((block_map, block_vec), "tm", combine, identity)
    lam_end = matmul(prefix[0], terminal) + prefix[1]
    states = []
    lam = lam_end
    for time_increment in range(steps_here - 1, -1, -1):
        lam = matmul(step_ops[time_increment], lam) + sources[time_increment]
        states.append(lam)
    adjoint_states = jnp.stack(states[::-1], axis=0)
    columns = lax.broadcasted_iota(jnp.int32, (gen_bus.shape[0], width), 1)
    selector = (columns == gen_bus[:, None]).astype(jnp.float32)
    picked = matmul(adjoint_states, selector.T)
    share = jnp.sum(picked * inertia_jac, axis=0)
    total = lax.psum(share, "tm")
    total_steps = steps_here * lax.axis_size("tm")
    sensitivity = total * float(total_steps) ** (-0.5)
    return (adjoint_states, sensitivity)


def solution(mesh):
    in_specs = (P("tm", None, None), P("tm", None), P(), P("tm", None), P())
    out_specs = (P("tm", None), P())
    return jax.shard_map(
        on_device, mesh=mesh, in_specs=in_specs, out_specs=out_specs, check_vma=False
    )
```

profile of v0, /device:TPU:1, one launch (start us, length us, event | category | flops | bytes accessed | tf_op | source)
XLA Modules:
  0.0 1046.5 jit_solution(16165328054481829497)
XLA Ops:
  7.2 2.1 fusion.10
  11.4 67.2 %all-gather.2 = f32[256,1,256]{2,1,0:T(1,128)S(1)} all-gather(f32[1,1,256]{2,1,0:T(1,128)S(1)} %bitcast.72), channel_id=3, replica_groups=mesh['tm'=256] {'tm'}, dimensions={0}, use_global_device_ids=true | all-gather | bytes 263168 | tf_op jit(solution)/shard_map/all_gather | solution.py:9
  78.8 149.0 %all-gather.5.cloned.1.call-done = f32[65536,256]{1,0:T(8,128)} async-done(((f32[256,256]{1,0:T(8,128)}), f32[65536,256]{1,0:T(8,128)}) %all-gather.5.cloned.1.call-update) | async-done | bytes 67108880 | tf_op jit(solution)/shard_map/all_gather | solution.py:9
  227.8 44.2 %rev.6 = f32[256,256,256]{2,1,0:T(8,128)} reverse(f32[256,256,256]{2,1,0:T(8,128)} %bitcast.2), dimensions={0} | reverse | bytes 134217728 | tf_op jit(solution)/shard_map/rev | solution.py:10
  272.0 691.4 %while.16 = (s32[]{:T(128)}, f32[256,256]{1,0:T(8,128)S(1)}, f32[256]{0:T(256)S(1)}, s32[]{:T(128)}, f32[256,256,256]{2,1,0:T(8,128)}, /*index=5*/f32[256,256]{1,0:T(8,128)S(1)}, s32[]{:T(128)}, s32[]{:T(128)}) while((s32[]{:T(128)}, f32[256,256]{1,0:T(8,128)S(1)}, f32[256]{0:T(256)S(1)}, s32[]{:T(128)}, ...), condition=%wide.region_1.2_spmd.clone, body=%wide.region_0.1_spmd.clone.sunk | while | flops 202179584 | bytes 1845375 | solution.py:20
  272.1 1.3 convolution_select_fusion.2
  293.8 1.3 convolution_select_fusion.2
  296.5 1.3 convolution_select_fusion.2
  299.2 1.3 convolution_select_fusion.2
  301.9 1.3 convolution_select_fusion.2
  304.6 1.3 convolution_select_fusion.2
  307.3 1.3 convolution_select_fusion.2
  345.3 1.3 convolution_select_fusion.2
  348.0 1.3 convolution_select_fusion.2
  350.7 1.3 convolution_select_fusion.2
  353.4 1.3 convolution_select_fusion.2
  356.1 1.3 convolution_select_fusion.2
  358.8 1.3 convolution_select_fusion.2
  396.8 1.3 convolution_select_fusion.2
  399.5 1.3 convolution_select_fusion.2
  402.2 1.3 convolution_select_fusion.2
  404.9 1.3 convolution_select_fusion.2
  407.6 1.3 convolution_select_fusion.2
  410.4 1.3 convolution_select_fusion.2
  448.3 1.3 convolution_select_fusion.2
  451.0 1.3 convolution_select_fusion.2
  453.7 1.3 convolution_select_fusion.2
  456.5 1.3 convolution_select_fusion.2
  459.2 1.3 convolution_select_fusion.2
  461.9 1.3 convolution_select_fusion.2
  499.8 1.3 convolution_select_fusion.2
  502.6 1.3 convolution_select_fusion.2
  505.3 1.3 convolution_select_fusion.2
  508.0 1.3 convolution_select_fusion.2
  510.7 1.3 convolution_select_fusion.2
  513.4 1.3 convolution_select_fusion.2
  551.4 1.3 convolution_select_fusion.2
  554.1 1.3 convolution_select_fusion.2
  556.8 1.3 convolution_select_fusion.2
  559.5 1.3 convolution_select_fusion.2
  562.2 1.3 convolution_select_fusion.2
  564.9 1.3 convolution_select_fusion.2
  602.9 1.3 convolution_select_fusion.2
  605.6 1.3 convolution_select_fusion.2
  608.3 1.3 convolution_select_fusion.2
  611.0 1.3 convolution_select_fusion.2
  613.7 1.3 convolution_select_fusion.2
  964.8 74.4 %psum.7 = f32[64]{0:T(128)S(1)} all-reduce(f32[64]{0:T(128)S(1)} %fusion.7), channel_id=1, replica_groups=mesh['tm'=256] {'tm'}, use_global_device_ids=true, to_apply=%region_3.4 | all-reduce | flops 64 | bytes 512 | tf_op jit(solution)/shard_map/psum | solution.py:52
  (1516 shorter events, 624.2 us)
Async XLA Ops:
  7.2 956.3 %copy-start = (f32[256]{0:T(256)S(1)}, f32[256]{0:T(256)}, u32[]{:S(2)}) copy-start(f32[256]{0:T(256)} %param.9) | copy-start | bytes 3076
  7.2 220.6 %all-gather.5.cloned.1.call-start = ((), (), s32[]{:S(2)}) async-start(), calls=%async_computation | async-start | bytes 67371008 | tf_op jit(solution)/shard_map/all_gather | solution.py:9
  227.8 736.0 %copy-start.1 = (f32[2,256,256]{2,1,0:T(8,128)S(1)}, f32[2,256,256]{2,1,0:T(8,128)}, u32[]{:S(2)}) copy-start(f32[2,256,256]{2,1,0:T(8,128)} %param.7) | copy-start | bytes 1572868
  227.8 736.7 %copy-start.3 = (f32[2,64]{1,0:T(2,128)S(1)}, f32[2,64]{1,0:T(2,128)}, u32[]{:S(2)}) copy-start(f32[2,64]{1,0:T(2,128)} %param.10) | copy-start | bytes 1540
  227.8 736.7 %copy-start.4 = (s32[64]{0:T(128)S(1)}, s32[64]{0:T(128)}, u32[]{:S(2)}) copy-start(s32[64]{0:T(128)} %param.11) | copy-start | bytes 772
  964.5 75.1 %copy-start.2 = (f32[2,256]{1,0:T(2,128)}, f32[2,256]{1,0:T(2,128)S(1)}, u32[]{:S(2)}) copy-start(f32[2,256]{1,0:T(2,128)S(1)} %pad_maximum_fusion) | copy-start | bytes 6148
Sparse Core Ops, SparseCore 0:
  11.6 216.1 all-gather.4
where the time goes:
time: 1060 us; the launch traced here: 1050 us
  matrix products  656 us (62%)
  waiting for transfers between devices  149 us (14%)
  blocking collectives  142 us (13%)
  local copies, waits for them, and re-layouts  65.5 us (6%)
  loops' own time  15.3 us (1%)
  between operations  14.2 us (1%)
    dot_general x516, matrix products, matmul(): jnp.dot(left, right, precision=lax.Precision.HIGHEST, preferred_element_t...  656 us
    all_gather x1, waiting for transfers between devices, prefix_2(): pieces = jax.tree.map(lambda part: lax.all_gather(part, axis), value)  149 us
    psum x1, blocking collectives, on_device(): total = lax.psum(share, 'tm')  74.4 us
    all_gather x1, blocking collectives, prefix_2(): pieces = jax.tree.map(lambda part: lax.all_gather(part, axis), value)  67.2 us
    rev x2, local copies, waits for them, and re-layouts, prefix_2(): pieces = jax.tree.map(lambda part: part[::-1], pieces)  44.4 us
  transfers between devices with their start and end apart: 1, of which 1 were waited for; matrix products, arithmetic and copies ran while one was open for 0% of the time, Pallas kernels for 0%

commit v1 on v0

--- a/solution.py
+++ b/solution.py
@@ -2,6 +2,11 @@
 import jax.numpy as jnp
 from jax import lax
 from jax.sharding import PartitionSpec as P
+from jax.lax import all_gather
+
+
+def switch_set(frame_in):
+    return all_gather(frame_in, axis_name="tm").sum(axis=0)
 
 
 def prefix_2(value, axis, join, neutral):
@@ -49,7 +54,7 @@
     selector = (columns == gen_bus[:, None]).astype(jnp.float32)
     picked = matmul(adjoint_states, selector.T)
     share = jnp.sum(picked * inertia_jac, axis=0)
-    total = lax.psum(share, "tm")
+    total = switch_set(share)
     total_steps = steps_here * lax.axis_size("tm")
     sensitivity = total * float(total_steps) ** (-0.5)
     return (adjoint_states, sensitivity)

time: 1060 us -> 1230 us (1.16)
  waiting for transfers between devices: 149 us -> 388 us
  blocking collectives: 142 us -> 67.1 us
    unnamed x1 -> x3, waiting for transfers between devices: 0.02 us -> 239 us
    psum x1 -> x0, blocking collectives: 74.4 us -> none  [on_device(): total = lax.psum(share, 'tm')]
  transfers between devices with their start and end apart: 1 -> 2, of which waited for: 1 -> 2; matrix products, arithmetic and copies ran while one was open for 0% -> 0% of each run, Pallas kernels for 0% -> 0%
where the time goes in v1:
time: 1230 us; the launch traced here: 1210 us
  matrix products  656 us (53%)
  waiting for transfers between devices  388 us (32%)
  local copies, waits for them, and re-layouts  67.3 us (5%)
  blocking collectives  67.1 us (5%)
  loops' own time  15.1 us (1%)
  between operations  14.2 us (1%)
    dot_general x516, matrix products, matmul(): jnp.dot(left, right, precision=lax.Precision.HIGHEST, preferred_element_t...  656 us
    unnamed x3, waiting for transfers between devices  239 us
    all_gather x1, waiting for transfers between devices, prefix_2(): pieces = jax.tree.map(lambda part: lax.all_gather(part, axis), value)  149 us
    all_gather x1, blocking collectives, prefix_2(): pieces = jax.tree.map(lambda part: lax.all_gather(part, axis), value)  67.1 us
    rev x2, local copies, waits for them, and re-layouts, prefix_2(): pieces = jax.tree.map(lambda part: part[::-1], pieces)  44.3 us
  transfers between devices with their start and end apart: 2, of which 2 were waited for; matrix products, arithmetic and copies ran while one was open for 0% of the time, Pallas kernels for 0%

profile of v1, /device:TPU:1, one launch (start us, length us, event | category | flops | bytes accessed | tf_op | source)
XLA Modules:
  0.0 1212.6 jit_solution(10227122875759349351)
XLA Ops:
  7.2 2.1 fusion.10
  11.5 67.1 %all-gather.3 = f32[256,1,256]{2,1,0:T(1,128)S(1)} all-gather(f32[1,1,256]{2,1,0:T(1,128)S(1)} %bitcast.72), channel_id=3, replica_groups=mesh['tm'=256] {'tm'}, dimensions={0}, use_global_device_ids=true | all-gather | bytes 263168 | tf_op jit(solution)/shard_map/all_gather | solution.py:14
  78.8 149.0 %all-gather.6.cloned.1.call-done = f32[65536,256]{1,0:T(8,128)} async-done(((f32[256,256]{1,0:T(8,128)}), f32[65536,256]{1,0:T(8,128)}) %all-gather.6.cloned.1.call-update) | async-done | bytes 67108880 | tf_op jit(solution)/shard_map/all_gather | solution.py:14
  227.8 44.2 %rev.6 = f32[256,256,256]{2,1,0:T(8,128)} reverse(f32[256,256,256]{2,1,0:T(8,128)} %bitcast.2), dimensions={0} | reverse | bytes 134217728 | tf_op jit(solution)/shard_map/rev | solution.py:15
  272.0 691.4 %while.16 = (s32[]{:T(128)}, f32[256,256]{1,0:T(8,128)S(1)}, f32[256]{0:T(256)S(1)}, s32[]{:T(128)}, f32[256,256,256]{2,1,0:T(8,128)}, /*index=5*/f32[256,256]{1,0:T(8,128)S(1)}, s32[]{:T(128)}, s32[]{:T(128)}) while((s32[]{:T(128)}, f32[256,256]{1,0:T(8,128)S(1)}, f32[256]{0:T(256)S(1)}, s32[]{:T(128)}, ...), condition=%wide.region_1.2_spmd.clone, body=%wide.region_0.1_spmd.clone.sunk | while | flops 202179584 | bytes 1845375 | solution.py:25
  272.1 1.3 convolution_select_fusion.2
  274.8 1.3 convolution_select_fusion.2
  285.6 1.3 convolution_select_fusion.2
  291.0 1.3 convolution_select_fusion.2
  296.5 1.3 convolution_select_fusion.2
  301.9 1.3 convolution_select_fusion.2
  307.3 1.3 convolution_select_fusion.2
  312.7 1.3 convolution_select_fusion.2
  318.2 1.3 convolution_select_fusion.2
  323.6 1.3 convolution_select_fusion.2
  329.0 1.3 convolution_select_fusion.2
  334.4 1.3 convolution_select_fusion.2
  339.9 1.3 convolution_select_fusion.2
  345.3 1.3 convolution_select_fusion.2
  350.7 1.3 convolution_select_fusion.2
  356.1 1.3 convolution_select_fusion.2
  361.5 1.3 convolution_select_fusion.2
  367.0 1.3 convolution_select_fusion.2
  372.4 1.3 convolution_select_fusion.2
  377.8 1.3 convolution_select_fusion.2
  388.7 1.3 convolution_select_fusion.2
  394.1 1.3 convolution_select_fusion.2
  399.5 1.3 convolution_select_fusion.2
  404.9 1.3 convolution_select_fusion.2
  410.4 1.3 convolution_select_fusion.2
  415.8 1.3 convolution_select_fusion.2
  421.2 1.3 convolution_select_fusion.2
  426.6 1.3 convolution_select_fusion.2
  432.0 1.3 convolution_select_fusion.2
  437.5 1.3 convolution_select_fusion.2
  442.9 1.3 convolution_select_fusion.2
  448.3 1.3 convolution_select_fusion.2
  453.7 1.3 convolution_select_fusion.2
  459.2 1.3 convolution_select_fusion.2
  464.6 1.3 convolution_select_fusion.2
  470.0 1.3 convolution_select_fusion.2
  475.4 1.3 convolution_select_fusion.2
  480.9 1.3 convolution_select_fusion.2
  491.7 1.3 convolution_select_fusion.2
  497.1 1.3 convolution_select_fusion.2
  502.5 1.3 convolution_select_fusion.2
  508.0 1.3 convolution_select_fusion.2
  965.7 238.5 %all-reduce.3.cloned.1.call-done = f32[16384]{0:T(1024)} async-done(((f32[16384]{0:T(1024)}), f32[16384]{0:T(1024)}) %all-reduce.3.cloned.1.call-update) | async-done | bytes 65552
  (1524 shorter events, 626.3 us)
Async XLA Ops:
  7.2 956.3 %copy-start = (f32[256]{0:T(256)S(1)}, f32[256]{0:T(256)}, u32[]{:S(2)}) copy-start(f32[256]{0:T(256)} %param.9) | copy-start | bytes 3076
  7.2 220.6 %all-gather.6.cloned.1.call-start = ((), (), s32[]{:S(2)}) async-start(), calls=%async_computation | async-start | bytes 67371008 | tf_op jit(solution)/shard_map/all_gather | solution.py:14
  9.4 1194.9 %all-reduce.3.cloned.1.call-start = ((), (), s32[]{:S(2)}) async-start(), calls=%async_computation.1 | async-start | bytes 131072
  227.8 736.0 %copy-start.1 = (f32[2,256,256]{2,1,0:T(8,128)S(1)}, f32[2,256,256]{2,1,0:T(8,128)}, u32[]{:S(2)}) copy-start(f32[2,256,256]{2,1,0:T(8,128)} %param.7) | copy-start | bytes 1572868
  227.8 736.7 %copy-start.4 = (f32[2,64]{1,0:T(2,128)S(1)}, f32[2,64]{1,0:T(2,128)}, u32[]{:S(2)}) copy-start(f32[2,64]{1,0:T(2,128)} %param.10) | copy-start | bytes 1540
  227.8 736.7 %copy-start.5 = (s32[64]{0:T(128)S(1)}, s32[64]{0:T(128)}, u32[]{:S(2)}) copy-start(s32[64]{0:T(128)} %param.11) | copy-start | bytes 772
  964.5 241.2 %copy-start.3 = (f32[2,256]{1,0:T(2,128)}, f32[2,256]{1,0:T(2,128)S(1)}, u32[]{:S(2)}) copy-start(f32[2,256]{1,0:T(2,128)S(1)} %pad_maximum_fusion) | copy-start | bytes 6148
  965.0 0.6 copy-start.2
Sparse Core Ops, SparseCore 0:
  11.6 216.1 all-gather.5
  965.8 238.3 all-reduce.2
